TPU v7x, 128 devices: a whole 4x4x4 slice. The times are simulated.
128 devices in a mesh: seq: 16 (over x, y_hi, core), tp: 8 (over z, y_lo).
Axes of the slice: x: 4, y: 4 (y_hi: 2, y_lo: 2; y = y_hi * 2 + y_lo), z: 4, core: 2. Of those that a mesh axis runs over, the one named last changes fastest.
Arguments:
- byte_ids: int32 [4096, 8], P('seq'), may hold values from 0 to 255
- global_out: bfloat16 [4096, 8192], P('seq', 'tp'), may hold values from -6 to 6
- global_in_grad: bfloat16 [4096, 8192], P('seq', 'tp'), may hold values from -6 to 6
- out_grad: bfloat16 [32768, 1024], P(('seq', 'tp')), may hold values from -6 to 6
- proj_weight: bfloat16 [1024, 1024], replicated, may hold values from -0.1875 to 0.1875
- emb_local: bfloat16 [256, 1024], replicated, may hold values from -6 to 6
- norm_gain: float32 [1024], replicated, may hold values from 0.1 to 1.9
- up_weight: bfloat16 [1024, 2048], replicated, may hold values from -0.1875 to 0.1875
- down_weight: bfloat16 [2048, 1024], replicated, may hold values from -0.125 to 0.125
Outputs:
- glob_out_grad: bfloat16 [4096, 8192], P('seq', 'tp')
- emb_global_grad: float32 [256, 1024], replicated
- emb_local_grad: float32 [256, 1024], replicated
- gain_grad: float32 [1024], replicated
- proj_grad: float32 [1024, 1024], P(None, ('seq', 'tp'))
- up_grad: float32 [1024, 2048], P(None, ('seq', 'tp'))
- down_grad: float32 [2048, 1024], P(('seq', 'tp'))
All inputs are finite; a program needn't handle non-finite values.
Results may differ from a plain program's by a relative error of at most 0.015.
Values may be sent and summed in bfloat16 or wider, within the bound.
A program may use at most 128 MiB of HBM per device.

v0:
```python
import jax
import jax.numpy as jnp
from jax import lax
from jax.sharding import PartitionSpec as P


def inner(left, right):
    return lax.dot_general(
        left, right, (((0,), (0,)), ((), ())), preferred_element_type=jnp.float32
    )


def outer(left, right):
    return lax.dot_general(
        left, right, (((1,), (1,)), ((), ())), preferred_element_type=jnp.float32
    )


def on_device(
    byte_ids,
    global_out,
    global_in_grad,
    out_grad,
    proj_weight,
    emb_local,
    norm_gain,
    up_weight,
    down_weight,
):
    tp_count = lax.axis_size("tp")
    tp_place = lax.axis_index("tp")
    patch = byte_ids.shape[1]
    slot = proj_weight.shape[0]
    vocab = emb_local.shape[0]
    local_patches = global_out.shape[0] // tp_count
    local_ids = lax.dynamic_slice_in_dim(byte_ids, tp_place * local_patches, local_patches, 0)
    local_out = lax.all_to_all(global_out, "tp", split_axis=0, concat_axis=1, tiled=True)
    slot_in = local_out.reshape(local_patches * patch, slot)
    first = jnp.full((local_patches, 1), -1, jnp.int32)
    prev_id = jnp.concatenate([first, local_ids[:, :-1]], axis=1).reshape(-1)
    prev_hot = jax.nn.one_hot(prev_id, vocab, dtype=jnp.bfloat16)
    u_rows = jnp.dot(slot_in, proj_weight, preferred_element_type=jnp.float32) + jnp.dot(
        prev_hot, emb_local, preferred_element_type=jnp.float32
    )
    scale = lax.rsqrt(jnp.mean(u_rows * u_rows, axis=1, keepdims=True) + 1e-05)
    normed = u_rows * scale
    r_rows = (normed * norm_gain).astype(jnp.bfloat16)
    a_rows = jnp.dot(r_rows, up_weight, preferred_element_type=jnp.float32)
    sig = jax.nn.sigmoid(a_rows)
    h_rows = (a_rows * sig).astype(jnp.bfloat16)
    dh_rows = outer(out_grad, down_weight)
    da_rows = (dh_rows * sig * (1.0 + a_rows * (1.0 - sig))).astype(jnp.bfloat16)
    dr_rows = outer(da_rows, up_weight)
    dn_rows = dr_rows * norm_gain
    du_rows = (
        out_grad.astype(jnp.float32)
        + scale * (dn_rows - normed * jnp.mean(dn_rows * normed, axis=1, keepdims=True))
    ).astype(jnp.bfloat16)
    local_back = (
        outer(du_rows, proj_weight).astype(jnp.bfloat16).reshape(local_patches, patch * slot)
    )
    glob_out_grad = lax.all_to_all(local_back, "tp", split_axis=1, concat_axis=0, tiled=True)
    slots_here = patch // tp_count
    own_ids = lax.dynamic_slice_in_dim(byte_ids, tp_place * slots_here, slots_here, 1).reshape(-1)
    own_hot = jax.nn.one_hot(own_ids, vocab, dtype=jnp.bfloat16)
    emb_global_part = inner(own_hot, global_in_grad)
    emb_local_part = inner(prev_hot, du_rows)
    gain_part = jnp.sum(dr_rows * normed, axis=0)
    emb_global_grad, emb_local_grad, gain_grad = lax.psum(
        (emb_global_part, emb_local_part, gain_part), ("seq", "tp")
    )
    proj_part = inner(slot_in, du_rows)
    up_part = inner(r_rows, da_rows)
    down_part = inner(h_rows, out_grad)
    proj_grad, up_grad, down_grad = (
        lax.psum_scatter(proj_part, ("seq", "tp"), scatter_dimension=1, tiled=True),
        lax.psum_scatter(up_part, ("seq", "tp"), scatter_dimension=1, tiled=True),
        lax.psum_scatter(down_part, ("seq", "tp"), scatter_dimension=0, tiled=True),
    )
    return (
        glob_out_grad,
        emb_global_grad,
        emb_local_grad,
        gain_grad,
        proj_grad,
        up_grad,
        down_grad,
    )


def solution(mesh):
    placed = (
        P("seq", None),
        P("seq", "tp"),
        P("seq", "tp"),
        P(("seq", "tp"), None),
        P(),
        P(),
        P(),
        P(),
        P(),
    )
    return jax.shard_map(
        on_device,
        mesh=mesh,
        in_specs=placed,
        out_specs=(
            P("seq", "tp"),
            P(),
            P(),
            P(),
            P(None, ("seq", "tp")),
            P(None, ("seq", "tp")),
            P(("seq", "tp"), None),
        ),
        check_vma=False,
    )
```

profile of v0, /device:TPU:0, one launch (start us, length us, event | category | flops | bytes accessed | tf_op | source)
XLA Modules:
  0.0 2162.4 jit_solution(6053280185825184937)
XLA Ops:
  7.2 6.6 all-to-all-start
  13.8 0.8 constant_dynamic-slice_fusion.1
  14.8 0.7 constant_dynamic-slice_fusion
  15.5 2.4 fusion.11
  18.0 5.9 all-to-all-done
  23.8 0.8 copy-done.1
  24.6 0.8 fusion.6
  25.5 0.4 multiply_reduce_fusion.2
  25.9 0.9 copy-done.4
  26.9 1.3 fusion.17
  28.2 1.0 copy-done.12
  29.2 1.5 fusion.1
  30.8 1.5 multiply_reduce_fusion
  32.3 0.3 add_convert_fusion
  32.6 0.8 copy-done.2
  33.4 1.4 fusion.10
  34.9 4.0 convolution_bitcast_fusion
  39.0 5.8 fusion.16
  44.8 1.0 copy-done.10
  45.8 6.2 fusion.3
  52.0 1.0 copy-done.3
  53.1 0.7 fusion.2
  53.8 1.1 copy.24
  54.9 3.5 all-to-all-start.1
  58.4 66.5 %psum.23 = f32[1024]{0:T(1024)} all-reduce(f32[1024]{0:T(1024)S(1)} %get-tuple-element.7), channel_id=1, replica_groups=mesh['seq'=16,'tp'=8] {'seq','tp'}, use_global_device_ids=true, to_apply=%region_5.6 | all-reduce | flops 1024 | bytes 8192 | tf_op jit(solution)/shard_map/psum | solution.py:69
  124.9 62.7 %all-reduce.4.cloned.1.call-done = (f32[256,1024]{1,0:T(8,128)}, f32[256,1024]{1,0:T(8,128)}) async-done(((f32[256,1024]{1,0:T(8,128)}, f32[256,1024]{1,0:T(8,128)}), (f32[256,1024]{1,0:T(8,128)}, f32[256,1024]{1,0:T(8,128)})) %all-reduce.4.cloned.1.call-update) | async-done | bytes 2097168 | tf_op jit(solution)/shard_map/psum | solution.py:69
  187.7 651.5 %reduce-scatter.4.cloned.1.call-done = f32[1024,8]{0,1:T(8,128)} async-done(((f32[1024,1024]{0,1:T(8,128)}), f32[1024,8]{0,1:T(8,128)}) %reduce-scatter.4.cloned.1.call-update) | async-done | bytes 32784 | tf_op jit(solution)/shard_map/reduce_scatter | solution.py:76
  839.2 656.4 %reduce-scatter.6.cloned.1.call-done = f32[1024,16]{0,1:T(8,128)} async-done(((f32[1024,2048]{0,1:T(8,128)}), f32[1024,16]{0,1:T(8,128)}) %reduce-scatter.6.cloned.1.call-update) | async-done | bytes 65552 | tf_op jit(solution)/shard_map/reduce_scatter | solution.py:77
  1495.7 656.1 %reduce-scatter.8.cloned.1.call-done = f32[16,1024]{1,0:T(8,128)} async-done(((f32[2048,1024]{1,0:T(8,128)}), f32[16,1024]{1,0:T(8,128)}) %reduce-scatter.8.cloned.1.call-update) | async-done | bytes 65552 | tf_op jit(solution)/shard_map/reduce_scatter | solution.py:78
  2151.8 0.8 copy.37
  2152.6 2.3 copy.38
  2154.9 1.0 copy.39
  (34 shorter events, 0.5 us)
Async XLA Ops:
  7.2 17.5 copy-start
  7.2 16.7 all-to-all-start
  13.8 173.9 %all-reduce.4.cloned.1.call-start = ((), (), s32[]{:S(2)}) async-start(), calls=%async_computation.8 | async-start | bytes 4194304 | tf_op jit(solution)/shard_map/psum | solution.py:69
  23.8 0.8 copy-start.1
  23.8 1.6 copy-start.8
  24.6 2.2 copy-start.4
  25.5 1.4 copy-start.11
  26.9 1.3 copy-start.9
  26.9 2.4 copy-start.12
  29.2 1.6 copy-start.5
  30.8 1.5 copy-start.6
  32.6 0.8 copy-start.2
  34.8 804.4 %reduce-scatter.4.cloned.1.call-start = ((), (), s32[]{:S(2)}) async-start(), calls=%async_computation.5 | async-start | bytes 4227072 | tf_op jit(solution)/shard_map/reduce_scatter | solution.py:76
  38.9 1456.8 %reduce-scatter.6.cloned.1.call-start = ((), (), s32[]{:S(2)}) async-start(), calls=%async_computation.6 | async-start | bytes 8454144 | tf_op jit(solution)/shard_map/reduce_scatter | solution.py:77
  44.8 1.0 copy-start.10
  44.8 2107.0 %reduce-scatter.8.cloned.1.call-start = ((), (), s32[]{:S(2)}) async-start(), calls=%async_computation.7 | async-start | bytes 8454144 | tf_op jit(solution)/shard_map/reduce_scatter | solution.py:78
  52.0 1.0 copy-start.3
  54.9 70.0 %all-to-all-start.1 = ((bf16[32,8,1024]{2,0,1:T(8,128)(2,1)}), bf16[32,8,1024]{2,0,1:T(8,128)(2,1)S(1)}, u32[]{:S(2)}, u32[]{:S(2)}) async-start(bf16[32,8,1024]{2,0,1:T(8,128)(2,1)} %copy.24), calls=%async_computation.1 | async-start | bytes 1048576 | tf_op jit(solution)/shard_map/all_to_all | solution.py:62
  2151.8 3.1 copy-start.7
Sparse Core Ops, SparseCore 0:
  35.0 152.6 all-reduce.3
  190.6 648.5 reduce-scatter.3
  842.2 653.4 reduce-scatter.5
  1498.5 653.3 reduce-scatter.7
where the time goes:
time: 2160 us
  waiting for transfers between devices  2030 us (94%)
  blocking collectives  66.5 us (3%)
  matrix products  26.2 us (1%)
    reduce_scatter x1, waiting for transfers between devices, on_device(): lax.psum_scatter(up_part, ('seq', 'tp'), scatter_dimension=1, tiled=True)  656 us
    reduce_scatter x1, waiting for transfers between devices, on_device(): lax.psum_scatter(down_part, ('seq', 'tp'), scatter_dimension=0, tiled=True)  656 us
    reduce_scatter x1, waiting for transfers between devices, on_device(): lax.psum_scatter(proj_part, ('seq', 'tp'), scatter_dimension=1, tiled=True)  652 us
    psum x1, blocking collectives, on_device(): lax.psum((emb_global_part, emb_local_part, gain_part), ('seq', 'tp'))  66.5 us
    psum x1, waiting for transfers between devices, on_device(): lax.psum((emb_global_part, emb_local_part, gain_part), ('seq', 'tp'))  62.7 us
  transfers between devices with their start and end apart: 6, of which 5 were waited for; matrix products, arithmetic and copies ran while one was open for 1% of the time, Pallas kernels for 0%

commit v1 on v0

--- a/solution.py
+++ b/solution.py
@@ -67,7 +67,7 @@
     emb_local_part = inner(prev_hot, du_rows)
     gain_part = jnp.sum(dr_rows * normed, axis=0)
     emb_global_grad, emb_local_grad, gain_grad = lax.psum(
-        (emb_global_part, emb_local_part, gain_part), ("seq", "tp")
+        lax.psum((emb_global_part, emb_local_part, gain_part), "tp"), "seq"
     )
     proj_part = inner(slot_in, du_rows)
     up_part = inner(r_rows, da_rows)

time: 2160 us -> 2120 us (0.981)
  waiting for transfers between devices: 2030 us -> 2000 us
    reduce_scatter x1, waiting for transfers between devices: 652 us -> 509 us  [on_device(): lax.psum_scatter(proj_part, ('seq', 'tp'), scatter_dimension=1, tiled=True)]
    psum x1 -> x2, waiting for transfers between devices: 62.7 us -> 169 us  [the longest x1 104 us: on_device(): lax.psum((emb_global_part, emb_local_part, gain_part), 'tp')]
    psum x1 -> x2, blocking collectives: 66.5 us -> 59.2 us  [the longest x1 33.9 us: on_device(): lax.psum(lax.psum((emb_global_part, emb_local_part, gain_part), 'tp'), 's...]
  transfers between devices with their start and end apart: 6 -> 7, of which waited for: 5 -> 6; matrix products, arithmetic and copies ran while one was open for 1% -> 1% of each run, Pallas kernels for 0% -> 0%
where the time goes in v1:
time: 2120 us
  waiting for transfers between devices  2000 us (94%)
  blocking collectives  59.2 us (3%)
  matrix products  26.2 us (1%)
    reduce_scatter x1, waiting for transfers between devices, on_device(): lax.psum_scatter(up_part, ('seq', 'tp'), scatter_dimension=1, tiled=True)  656 us
    reduce_scatter x1, waiting for transfers between devices, on_device(): lax.psum_scatter(down_part, ('seq', 'tp'), scatter_dimension=0, tiled=True)  656 us
    reduce_scatter x1, waiting for transfers between devices, on_device(): lax.psum_scatter(proj_part, ('seq', 'tp'), scatter_dimension=1, tiled=True)  509 us
    psum x1, waiting for transfers between devices, on_device(): lax.psum((emb_global_part, emb_local_part, gain_part), 'tp')  104 us
    psum x1, waiting for transfers between devices, on_device(): lax.psum(lax.psum((emb_global_part, emb_local_part, gain_part), 'tp'), 's...  64.8 us
  transfers between devices with their start and end apart: 7, of which 6 were waited for; matrix products, arithmetic and copies ran while one was open for 1% of the time, Pallas kernels for 0%

profile of v1, /device:TPU:0, one launch (start us, length us, event | category | flops | bytes accessed | tf_op | source)
XLA Modules:
  0.0 2119.5 jit_solution(14036991199184751554)
XLA Ops:
  8.0 6.6 all-to-all-start
  14.6 0.8 constant_dynamic-slice_fusion.1
  15.7 0.7 constant_dynamic-slice_fusion
  16.4 2.4 fusion.11
  18.8 5.9 all-to-all-done
  24.7 0.8 copy-done.1
  25.5 0.8 fusion.6
  26.8 0.9 copy-done.4
  27.7 1.3 fusion.17
  29.0 1.0 copy-done.12
  30.1 1.5 fusion.1
  31.6 1.5 multiply_reduce_fusion
  33.5 0.8 copy-done.2
  34.3 1.4 fusion.10
  35.7 104.0 %all-reduce.8.cloned.1.call-done = (f32[256,1024]{1,0:T(8,128)}, f32[256,1024]{1,0:T(8,128)}) async-done(((f32[256,1024]{1,0:T(8,128)}, f32[256,1024]{1,0:T(8,128)}), (f32[256,1024]{1,0:T(8,128)}, f32[256,1024]{1,0:T(8,128)})) %all-reduce.8.cloned.1.call-update) | async-done | bytes 2097168 | tf_op jit(solution)/shard_map/psum | solution.py:70
  139.8 4.0 convolution_bitcast_fusion
  143.9 5.8 fusion.16
  149.8 1.0 copy-done.10
  150.7 6.2 fusion.3
  157.0 1.0 copy-done.3
  158.0 0.7 fusion.2
  158.7 1.1 copy.24
  159.8 3.5 all-to-all-start.1
  163.3 25.3 %psum.46 = f32[1024]{0:T(1024)S(1)} all-reduce(f32[1024]{0:T(1024)S(1)} %get-tuple-element.7), channel_id=1, replica_groups=mesh['seq'=16,'tp'=8] {'tp'}, use_global_device_ids=true, to_apply=%region_7.8 | all-reduce | flops 1024 | bytes 8192 | tf_op jit(solution)/shard_map/psum | solution.py:70
  188.6 33.9 %psum.47 = f32[1024]{0:T(1024)} all-reduce(f32[1024]{0:T(1024)S(1)} %psum.46), channel_id=1, replica_groups=mesh['seq'=16,'tp'=8] {'seq'}, use_global_device_ids=true, to_apply=%region_8.9 | all-reduce | flops 1024 | bytes 8192 | tf_op jit(solution)/shard_map/psum | solution.py:69
  222.5 64.8 %all-reduce.6.cloned.1.call-done = (f32[256,1024]{1,0:T(8,128)}, f32[256,1024]{1,0:T(8,128)}) async-done(((f32[256,1024]{1,0:T(8,128)}, f32[256,1024]{1,0:T(8,128)}), (f32[256,1024]{1,0:T(8,128)}, f32[256,1024]{1,0:T(8,128)})) %all-reduce.6.cloned.1.call-update) | async-done | bytes 2097168 | tf_op jit(solution)/shard_map/psum | solution.py:69
  287.3 508.8 %reduce-scatter.4.cloned.1.call-done = f32[1024,8]{0,1:T(8,128)} async-done(((f32[1024,1024]{0,1:T(8,128)}), f32[1024,8]{0,1:T(8,128)}) %reduce-scatter.4.cloned.1.call-update) | async-done | bytes 32784 | tf_op jit(solution)/shard_map/reduce_scatter | solution.py:76
  796.1 656.1 %reduce-scatter.6.cloned.1.call-done = f32[1024,16]{0,1:T(8,128)} async-done(((f32[1024,2048]{0,1:T(8,128)}), f32[1024,16]{0,1:T(8,128)}) %reduce-scatter.6.cloned.1.call-update) | async-done | bytes 65552 | tf_op jit(solution)/shard_map/reduce_scatter | solution.py:77
  1452.2 655.7 %reduce-scatter.8.cloned.1.call-done = f32[16,1024]{1,0:T(8,128)} async-done(((f32[2048,1024]{1,0:T(8,128)}), f32[16,1024]{1,0:T(8,128)}) %reduce-scatter.8.cloned.1.call-update) | async-done | bytes 65552 | tf_op jit(solution)/shard_map/reduce_scatter | solution.py:78
  2107.9 0.8 copy.39
  2108.7 2.3 copy.40
  2111.0 1.0 copy.41
  (38 shorter events, 1.3 us)
Async XLA Ops:
  8.0 17.5 copy-start
  8.0 16.7 all-to-all-start
  14.6 125.1 %all-reduce.8.cloned.1.call-start = ((), (), s32[]{:S(2)}) async-start(), calls=%async_computation.9 | async-start | bytes 4194304 | tf_op jit(solution)/shard_map/psum | solution.py:70
  24.7 0.8 copy-start.1
  24.7 1.6 copy-start.8
  25.5 2.2 copy-start.4
  26.3 1.4 copy-start.11
  27.7 1.3 copy-start.9
  27.7 2.4 copy-start.12
  30.1 1.6 copy-start.5
  31.6 1.5 copy-start.6
  33.5 0.8 copy-start.2
  35.7 251.6 %all-reduce.6.cloned.1.call-start = ((), (), s32[]{:S(2)}) async-start(), calls=%async_computation.8 | async-start | bytes 4194304 | tf_op jit(solution)/shard_map/psum | solution.py:69
  139.8 656.3 %reduce-scatter.4.cloned.1.call-start = ((), (), s32[]{:S(2)}) async-start(), calls=%async_computation.5 | async-start | bytes 4227072 | tf_op jit(solution)/shard_map/reduce_scatter | solution.py:76
  143.8 1308.3 %reduce-scatter.6.cloned.1.call-start = ((), (), s32[]{:S(2)}) async-start(), calls=%async_computation.6 | async-start | bytes 8454144 | tf_op jit(solution)/shard_map/reduce_scatter | solution.py:77
  149.7 1.1 copy-start.10
  149.7 1958.2 %reduce-scatter.8.cloned.1.call-start = ((), (), s32[]{:S(2)}) async-start(), calls=%async_computation.7 | async-start | bytes 8454144 | tf_op jit(solution)/shard_map/reduce_scatter | solution.py:78
  156.9 1.0 copy-start.3
  159.8 62.7 %all-to-all-start.1 = ((bf16[32,8,1024]{2,0,1:T(8,128)(2,1)}), bf16[32,8,1024]{2,0,1:T(8,128)(2,1)S(1)}, u32[]{:S(2)}, u32[]{:S(2)}) async-start(bf16[32,8,1024]{2,0,1:T(8,128)(2,1)} %copy.24), calls=%async_computation.1 | async-start | bytes 1048576 | tf_op jit(solution)/shard_map/all_to_all | solution.py:62
  2107.9 3.1 copy-start.7
Sparse Core Ops, SparseCore 0:
  35.8 103.8 all-reduce.7
  142.3 144.9 all-reduce.5
Sparse Core Ops, SparseCore 1:
  143.9 652.1 reduce-scatter.3
  798.9 653.2 reduce-scatter.5
  1455.0 652.8 reduce-scatter.7
